TPU v7x, 256 devices: a whole 4x4x8 slice. The times are simulated.
256 devices in a mesh: seq: 16 (over x, y), fsdp: 16 (over z, core).
Axes of the slice: x: 4, y: 4, z: 8, core: 2. Of those that a mesh axis runs over, the one named last changes fastest.
Arguments:
- patches: bfloat16 [16, 8704, 1176], P('fsdp', 'seq'), may hold values from -6 to 6
- send_slot: int32 [16, 272], P('fsdp', 'seq'), may hold values from 0 to 271, as said below
- segments: int32 [16, 272], P('fsdp'), may hold values from 0 to 33, never falling along the last dimension, each value on 1 to 24 neighbouring positions
- stem_weight: bfloat16 [3584, 1176], P('fsdp'), may hold values from -0.1875 to 0.1875
- norm_gain: bfloat16 [3584], P('fsdp'), may hold values from 0.099609375 to 1.8984375
- conv_kernel: bfloat16 [5, 3584], P(None, 'fsdp'), may hold values from -3 to 3
- cotangent: bfloat16 [16, 8704, 3584], P('fsdp', 'seq'), may hold values from -6 to 6
Outputs:
- features: bfloat16 [16, 8704, 3584], P('fsdp', 'seq')
- grad_patches: bfloat16 [16, 8704, 1176], P('fsdp', 'seq')
- grad_weight: bfloat16 [3584, 1176], P('fsdp')
- grad_channels: float32 [6, 3584], P(None, 'fsdp')
Inputs may be any that keep to these rules, and one draw needn't show every extreme that they name: `send_slot`: each row is a permutation of the packed slots. At most 2 frame slots of one device go to one device's packed slots, and every device sends exactly 2 to some device; within a row the number that device s sends to device (s + o) modulo the seq axis size depends on o alone. `segments`: ids never fall along a row; a clip holds 1 to 24 slots, one exactly 24.
All inputs are finite; a program needn't handle non-finite values.
Results may differ from a plain program's by a relative error of at most 0.0056.
Values may be sent and summed in bfloat16 or wider, within the bound.
A program may use at most 192 MiB of HBM per device.

v0:
```python
import math
import jax
import jax.numpy as jnp
from jax import lax
from jax.sharding import PartitionSpec as P

EPSILON = 1e-06


def pl_ceil(total, step):
    return -(-total // step)


def extended_2(cells, sides, width):
    for axis, dim in sides:
        count = lax.axis_size(axis)
        ends = count - 1
        head = lax.slice_in_dim(cells, 0, width, axis=dim)
        tail = lax.slice_in_dim(cells, cells.shape[dim] - width, cells.shape[dim], axis=dim)
        cells = jnp.concatenate(
            [
                lax.ppermute(tail, axis, [(i, (i + 1) % count) for i in range(ends)]),
                cells,
                lax.ppermute(head, axis, [((i + 1) % count, i) for i in range(ends)]),
            ],
            axis=dim,
        )
    return cells


def slot_mask(segment_row, centre):
    slot_total = segment_row.shape[0]
    safe_centre = jnp.clip(centre, 0, slot_total - 1)
    columns = []
    for offset in range(5):
        neighbour = centre + (offset - 2)
        inside = (neighbour >= 0) & (neighbour < slot_total) & (centre >= 0) & (centre < slot_total)
        same_clip = segment_row[jnp.clip(neighbour, 0, slot_total - 1)] == segment_row[safe_centre]
        columns.append((inside & same_clip).astype(jnp.float32))
    return jnp.stack(columns, axis=1)


def temporal_mix(padded, clip_mask, kernel, slot_total):
    kernel_wide = kernel.astype(jnp.float32)
    result = padded[0:slot_total].astype(jnp.float32) * (
        clip_mask[:, 0][:, None, None] * kernel_wide[0][None, None, :]
    )
    for offset in range(1, 5):
        addend = padded[offset : offset + slot_total].astype(jnp.float32) * (
            clip_mask[:, offset][:, None, None] * kernel_wide[offset][None, None, :]
        )
        result = result + addend
    return result


def temporal_back(slope_padded, mask_padded, kernel, slot_total):
    kernel_wide = kernel.astype(jnp.float32)
    result = jnp.zeros((slot_total,) + slope_padded.shape[1:], jnp.float32)
    for offset in range(5):
        first_row = 4 - offset
        weights_row = (
            mask_padded[first_row : first_row + slot_total, offset][:, None, None]
            * kernel_wide[offset][None, None, :]
        )
        result = (
            result
            + slope_padded[first_row : first_row + slot_total].astype(jnp.float32) * weights_row
        )
    return result


def kernel_sums(slope_blocks, padded, clip_mask, slot_total):
    stacked = []
    for offset in range(5):
        product = jnp.sum(
            slope_blocks.astype(jnp.float32)
            * padded[offset : offset + slot_total].astype(jnp.float32),
            axis=1,
        )
        stacked.append(jnp.sum(product * clip_mask[:, offset][:, None], axis=0))
    return jnp.stack(stacked, axis=0)


def rim_rows(values, margin):
    return extended_2(values, (("seq", 0),), margin)


def shards(patches, send_slot, segments, stem_weight, norm_gain, conv_kernel, cotangent):
    seq_size = lax.axis_size("seq")
    fsdp_size = lax.axis_size("fsdp")
    seq_index = lax.axis_index("seq")
    slot_count = send_slot.shape[1]
    tokens = patches.shape[1]
    slot_rows = tokens // slot_count
    pixel_width = patches.shape[2]
    capacity = 2 * slot_count // seq_size
    destination = send_slot[0]
    owner_index = destination // slot_count
    same_owner = owner_index[:, None] == owner_index[None, :]
    earlier = destination[None, :] < destination[:, None]
    ranking = jnp.sum((same_owner & earlier).astype(jnp.int32), axis=1)
    buffer_row = owner_index * capacity + ranking
    frames = patches[0].reshape(slot_count, slot_rows, pixel_width)
    outbox = (
        jnp.zeros((seq_size * capacity, slot_rows, pixel_width), jnp.bfloat16)
        .at[buffer_row]
        .set(frames)
    )
    position = (
        jnp.full((seq_size * capacity,), -1.0, jnp.float32)
        .at[buffer_row]
        .set((destination % slot_count).astype(jnp.float32))
        .astype(jnp.bfloat16)
    )
    incoming, arrived = (
        lax.all_to_all(outbox, "seq", split_axis=0, concat_axis=0, tiled=True),
        lax.all_to_all(position, "seq", split_axis=0, concat_axis=0, tiled=True),
    )
    arrived_float = arrived.astype(jnp.float32)
    target = jnp.where(arrived_float >= 0.0, arrived_float, float(slot_count)).astype(jnp.int32)
    packed = (
        jnp.zeros((slot_count + 1, slot_rows, pixel_width), jnp.bfloat16)
        .at[target]
        .set(incoming)[:slot_count]
        .reshape(tokens, pixel_width)
    )
    extras = jnp.concatenate([norm_gain[:, None], conv_kernel.T], axis=1)
    shard_ext = jnp.concatenate([stem_weight, extras], axis=1)
    gathered = lax.all_gather(shard_ext, "fsdp", axis=0, tiled=True)
    weight_full = gathered[:, :pixel_width]
    channel_low = gathered[:, pixel_width:].T
    gain_low = channel_low[0]
    kernel_full = channel_low[1:]
    gain_wide = gain_low.astype(jnp.float32)
    channels = weight_full.shape[0]
    stem_out = lax.dot_general(
        packed, weight_full, (((1,), (1,)), ((), ())), preferred_element_type=jnp.float32
    )
    inv_rms = lax.rsqrt(jnp.mean(stem_out * stem_out, axis=1, keepdims=True) + EPSILON)
    unit_rows = stem_out * inv_rms
    normed = (unit_rows * gain_wide).astype(jnp.bfloat16)
    segment_row = segments[0]
    centre = seq_index * slot_count + jnp.arange(slot_count, dtype=jnp.int32)
    extended = seq_index * slot_count + jnp.arange(-2, slot_count + 2, dtype=jnp.int32)
    clip_mask = slot_mask(segment_row, centre)
    mask_padded = slot_mask(segment_row, extended)
    padded = rim_rows(normed, 2 * slot_rows).reshape(slot_count + 4, slot_rows, channels)
    mixed_rows = temporal_mix(padded, clip_mask, kernel_full, slot_count).reshape(tokens, channels)
    features = (stem_out + jax.nn.silu(mixed_rows)).astype(jnp.bfloat16)
    upstream_wide = cotangent[0].astype(jnp.float32)
    gate_value = jax.nn.sigmoid(mixed_rows)
    slope_low = (upstream_wide * gate_value * (1.0 + mixed_rows * (1.0 - gate_value))).astype(
        jnp.bfloat16
    )
    slope_padded = rim_rows(slope_low, 2 * slot_rows).reshape(slot_count + 4, slot_rows, channels)
    d_normed = temporal_back(slope_padded, mask_padded, kernel_full, slot_count).reshape(
        tokens, channels
    )
    gated = d_normed * gain_wide
    d_stem = upstream_wide + inv_rms * (
        gated - unit_rows * jnp.mean(gated * unit_rows, axis=1, keepdims=True)
    )
    d_stem_low = d_stem.astype(jnp.bfloat16)
    grad_rows = jnp.dot(d_stem_low, weight_full, preferred_element_type=jnp.float32).astype(
        jnp.bfloat16
    )
    gain_part = jnp.sum(d_normed * unit_rows, axis=0)
    slope_blocks = slope_padded[2 : 2 + slot_count]
    kernel_part = kernel_sums(slope_blocks, padded, clip_mask, slot_count)
    chan_terms = jnp.concatenate([gain_part[None, :], kernel_part], axis=0).T
    weight_block = lax.dot_general(
        d_stem_low,
        jnp.pad(packed, ((0, 0), (0, 6))),
        (((0,), (0,)), ((), ())),
        preferred_element_type=jnp.float32,
    )
    total_block = weight_block + jnp.pad(chan_terms, ((0, 0), (pixel_width, 0)))
    panel = channels // fsdp_size
    panel_padded = 16 * seq_size * pl_ceil(panel, 16 * seq_size)
    stacked = jnp.pad(
        total_block.reshape(fsdp_size, panel, pixel_width + 6),
        ((0, 0), (0, panel_padded - panel), (0, 0)),
    ).reshape(fsdp_size * panel_padded, pixel_width + 6)
    piece = lax.psum_scatter(stacked, ("fsdp", "seq"), scatter_dimension=0, tiled=True)
    grad_scale = 1.0 / math.sqrt(tokens * seq_size * fsdp_size)
    summed = lax.all_gather(piece * grad_scale, "seq", axis=0, tiled=True)[:panel]
    grad_weight = summed[:, :pixel_width].astype(jnp.bfloat16)
    grad_channels = summed[:, pixel_width:].T
    return (features[None], grad_rows[None], grad_weight, grad_channels)


def solution(mesh):
    in_specs = (
        P("fsdp", "seq", None),
        P("fsdp", "seq"),
        P("fsdp", None),
        P("fsdp", None),
        P("fsdp"),
        P(None, "fsdp"),
        P("fsdp", "seq", None),
    )
    out_specs = (P("fsdp", "seq", None), P("fsdp", "seq", None), P("fsdp", None), P(None, "fsdp"))
    return jax.shard_map(shards, mesh=mesh, in_specs=in_specs, out_specs=out_specs, check_vma=False)
```

profile of v0, /device:TPU:1, one launch (start us, length us, event | category | flops | bytes accessed | tf_op | source)
XLA Modules:
  0.0 1608.6 jit_solution(15183071175365913867)
XLA Ops:
  7.2 0.7 broadcast_in_dim.26
  8.0 0.8 copy.34
  8.8 1.9 concatenate.24
  10.7 0.7 fusion.30
  11.4 0.7 fusion.31
  12.1 0.9 convert_reduce_fusion.1
  13.0 0.7 fusion.34
  13.7 0.6 scatter_custom_fusion
  14.3 0.7 all_to_all.12
  15.0 7.6 all-to-all-start
  22.8 1.8 broadcast_in_dim.21
  24.6 7.2 scatter_fusion
  31.9 6.7 all-to-all-start.1
  38.6 0.7 gather_fusion
  39.4 0.7 gather_fusion.5
  40.1 0.7 gather_fusion.1
  40.8 0.7 gather_fusion.2
  41.5 0.7 gather_fusion.3
  42.2 0.7 gather_fusion.4
  42.9 0.7 gather_fusion.7
  43.6 0.7 gather_fusion.6
  44.3 0.7 gather_fusion.8
  45.1 0.7 gather_fusion.9
  46.3 26.7 %all-to-all-done.1 = bf16[32,32,1176]{2,1,0:T(8,128)(2,1)} async-done(((bf16[32,32,1176]{2,1,0:T(8,128)(2,1)}), bf16[32,32,1176]{2,1,0:T(8,128)(2,1)}, u32[]{:S(2)}, u32[]{:S(2)}) %all-to-all-start.1) | async-done | bytes 2408480 | tf_op jit(solution)/shard_map/all_to_all | solution.py:116
  73.0 0.1 broadcast_in_dim.18
  73.1 4.6 scatter_fusion.1
  77.9 1.6 slice_bitcast_fusion
  79.5 0.3 convert_reduce_fusion
  79.9 0.3 slice_convert_fusion.1
  80.2 4.3 slice_reduce_fusion.4
  84.5 5.5 multiply_reduce_fusion.2
  90.0 1.3 multiply_convert_fusion
  91.4 2.6 collective-permute-start
  94.0 1.4 collective-permute-start.1
  95.6 0.8 broadcast_multiply_fusion
  96.4 0.9 broadcast_multiply_fusion.1
  97.3 0.9 broadcast_multiply_fusion.2
  98.2 0.9 broadcast_multiply_fusion.3
  99.0 1.4 collective-permute-done
  100.4 4.1 collective-permute-done.1
  104.6 19.6 %convert_multiply_fusion = (f32[544,3584]{1,0:T(8,128)}, bf16[544,3584]{1,0:T(8,128)(2,1)}, f32[544,3584]{1,0:T(8,128)}) fusion(bf16[64,3584]{1,0:T(8,128)(2,1)S(1)} %collective-permute-done.1, bf16[544,3584]{1,0:T(8,128)(2,1)S(1)} %multiply_convert_fusion, bf16[1,544,3584]{2,1,0:T(8,128)(2,1)S(1)} %copy-done.4, f32[17,3584]{1,0:T(8,128)S(1)} %get-tuple-element.57, ...), kind=kLoop, calls=%fused_computation.13 | loop fusion | flops 74088448 | bytes 29431808 | tf_op jit(solution)/shard_map/mul | solution.py:76
  124.2 4.3 reduce_sum.141
  128.7 2.0 fusion.54
  130.7 1.3 collective-permute-start.2
  131.9 4.8 collective-permute-start.3
  136.8 15.1 convert_multiply_fusion.1
  151.9 4.3 reduce_sum.139
  156.4 4.4 reduce_sum.137
  160.9 4.4 reduce_sum.133
  165.4 4.4 reduce_sum.135
  169.9 10.2 fusion.13
  180.2 2.1 multiply_reduce_fusion
  182.3 9.6 fusion.10
  192.0 0.1 concatenate.29
  192.1 13.7 pad_add_fusion
  205.8 18.8 %copy.35 = f32[3584,1182]{1,0:T(8,128)} copy(f32[3584,1182]{0,1:T(8,128)} %pad_add_fusion) | data formatting | bytes 33890304 | tf_op jit(solution)/shard_map/add | solution.py:177
  224.6 15.3 pad.14
  239.9 1284.5 %reduce-scatter.4.cloned.1.call-done = f32[16,1182]{1,0:T(8,128)} async-done(((f32[4096,1182]{1,0:T(8,128)}), f32[16,1182]{1,0:T(8,128)}) %reduce-scatter.4.cloned.1.call-update) | async-done | bytes 75664 | tf_op jit(solution)/shard_map/reduce_scatter | solution.py:184
  1524.4 1.5 broadcast_multiply_fusion.10
  1526.0 10.4 fusion.23
  1536.4 61.6 %all-gather.5.cloned.1.call-done = f32[256,1182]{1,0:T(8,128)} async-done(((f32[16,1182]{1,0:T(8,128)}), f32[256,1182]{1,0:T(8,128)}) %all-gather.5.cloned.1.call-update) | async-done | bytes 1210384 | tf_op jit(solution)/shard_map/all_gather | solution.py:186
  1598.0 1.0 slice_bitcast_fusion.1
  1599.0 0.7 copy.38
  1599.7 2.1 slice.292
  (75 shorter events, 1.8 us)
Async XLA Ops:
  7.2 31.5 %copy-start = (s32[1,272]{1,0:T(1,128)S(1)}, s32[1,272]{1,0:T(1,128)}, u32[]{:S(2)}) copy-start(s32[1,272]{1,0:T(1,128)} %param.9) | copy-start | bytes 3268
  7.2 70.7 %all-gather.3.cloned.1.call-start = ((), (), s32[]{:S(2)}) async-start(), calls=%async_computation.3 | async-start | bytes 9748480 | tf_op jit(solution)/shard_map/all_gather | solution.py:129
  15.0 16.9 %all-to-all-start = ((bf16[16,2,1]{1,2,0:T(2,128)(2,1)}), bf16[16,2,1]{1,2,0:T(2,128)(2,1)S(1)}, u32[]{:S(2)}, u32[]{:S(2)}) async-start(bf16[16,2,1]{1,2,0:T(2,128)(2,1)} %all_to_all.12), calls=%async_computation | async-start | bytes 16384 | tf_op jit(solution)/shard_map/all_to_all | solution.py:117
  31.9 41.1 %all-to-all-start.1 = ((bf16[32,32,1176]{2,1,0:T(8,128)(2,1)}), bf16[32,32,1176]{2,1,0:T(8,128)(2,1)}, u32[]{:S(2)}, u32[]{:S(2)}) async-start(bf16[32,32,1176]{2,1,0:T(8,128)(2,1)} %scatter_fusion), calls=%async_computation.1 | async-start | bytes 5242880 | tf_op jit(solution)/shard_map/all_to_all | solution.py:116
  38.5 1485.8 %reduce-scatter.4.cloned.1.call-start = ((), (), s32[]{:S(2)}) async-start(), calls=%async_computation.5 | async-start | bytes 21053440 | tf_op jit(solution)/shard_map/reduce_scatter | solution.py:184
  77.9 6.7 copy-start.5
  90.0 7.3 copy-start.2
  90.0 14.6 copy-start.4
  91.3 32.8 %copy-start.3 = (bf16[544,3584]{1,0:T(8,128)(2,1)}, bf16[544,3584]{1,0:T(8,128)(2,1)S(1)}, u32[]{:S(2)}) copy-start(bf16[544,3584]{1,0:T(8,128)(2,1)S(1)} %multiply_convert_fusion) | copy-start | bytes 11698180
  91.4 9.0 collective-permute-start
  94.0 10.5 collective-permute-start.1
  130.7 39.3 %collective-permute-start.2 = (bf16[64,3584]{1,0:T(8,128)(2,1)}, bf16[64,3584]{1,0:T(8,128)(2,1)}, u32[]{:S(2)}, u32[]{:S(2)}) collective-permute-start(bf16[64,3584]{1,0:T(8,128)(2,1)} %get-tuple-element.44), channel_id=1, source_target_pairs={{16,0},{32,16},{48,32},{64,48},{80,64},{96,80},{112,96},{128,112},... | collective-permute-start | bytes 1376264 | tf_op jit(solution)/shard_map/ppermute | solution.py:24
  131.9 38.0 %collective-permute-start.3 = (bf16[64,3584]{1,0:T(8,128)(2,1)S(1)}, bf16[64,3584]{1,0:T(8,128)(2,1)}, u32[]{:S(2)}, u32[]{:S(2)}) collective-permute-start(bf16[64,3584]{1,0:T(8,128)(2,1)S(1)} %get-tuple-element.45), channel_id=1, source_target_pairs={{0,16},{16,32},{32,48},{48,64},{64,80},{80,96},{96,112},{112,128},... | collective-permute-start | bytes 1376264 | tf_op jit(solution)/shard_map/ppermute | solution.py:22
  169.8 10.4 slice-start
  169.9 10.3 slice-start.1
  239.9 1358.1 %all-gather.5.cloned.1.call-start = ((), (), s32[]{:S(2)}) async-start(), calls=%async_computation.4 | async-start | bytes 1392640 | tf_op jit(solution)/shard_map/all_gather | solution.py:186
  1526.0 75.9 %copy-start.1 = (s32[1,272]{1,0:T(1,128)S(1)}, s32[1,272]{1,0:T(1,128)}, u32[]{:S(2)}) copy-start(s32[1,272]{1,0:T(1,128)} %param.9) | copy-start | bytes 3268
Sparse Core Ops, SparseCore 0:
  10.9 63.8 all-gather.2
  240.0 1284.3 reduce-scatter.3
  1527.5 70.5 all-gather.4
where the time goes:
time: 1610 us
  waiting for transfers between devices  1380 us (86%)
  other arithmetic  89.6 us (6%)
  local copies, waits for them, and re-layouts  72 us (4%)
  matrix products  29.6 us (2%)
  starting transfers between devices  24.5 us (2%)
    reduce_scatter x1, waiting for transfers between devices, shards(): lax.psum_scatter(stacked, ('fsdp', 'seq'), scatter_dimension=0, tiled=True)  1280 us
    all_gather x1, waiting for transfers between devices, shards(): lax.all_gather(piece * grad_scale, 'seq', axis=0, tiled=True)[:panel]  61.6 us
    mul x2, other arithmetic, kernel_sums(): slope_blocks.astype(jnp.float32)  34.7 us
  transfers between devices with their start and end apart: 9, of which 5 were waited for; matrix products, arithmetic and copies ran while one was open for 4% of the time, Pallas kernels for 0%

commit v1 on v0

--- a/solution.py
+++ b/solution.py
@@ -5,6 +5,16 @@
 from jax.sharding import PartitionSpec as P
 
 EPSILON = 1e-06
+
+
+def draw_pipes_on_mesh(mine_x, dimension_no):
+    mine_x = jnp.moveaxis(mine_x, 0, dimension_no)
+    far_arr = mine_x.shape
+    return mine_x.reshape(
+        *far_arr[:dimension_no],
+        far_arr[dimension_no] * far_arr[dimension_no + 1],
+        *far_arr[dimension_no + 2 :]
+    )
 
 
 def pl_ceil(total, step):
@@ -86,6 +96,28 @@
 
 
 def shards(patches, send_slot, segments, stem_weight, norm_gain, conv_kernel, cotangent):
+
+    def convert_ways(local_x, chip_axis, axis_k):
+        n_chips = jax.lax.axis_size(chip_axis)
+        pieces_in = list(map(lambda q: (q, (q + 1) % n_chips), range(n_chips)))
+        items = [(dev_j, dev) for dev, dev_j in pieces_in]
+        everything, after = ([], [])
+        num = 0
+        while num < n_chips - 1:
+            if num % 2 == 0:
+                everything.append(
+                    jax.lax.ppermute(
+                        everything[-1] if everything else local_x, chip_axis, pieces_in
+                    )
+                )
+            else:
+                after.append(jax.lax.ppermute(after[-1] if after else local_x, chip_axis, items))
+            num += 1
+        finding = jnp.stack([*everything[::-1], local_x, *after], axis=0)
+        res = jax.lax.axis_index(chip_axis) - len(everything)
+        finding = finding[(jnp.arange(n_chips) - res) % n_chips]
+        return draw_pipes_on_mesh(finding, axis_k)
+
     seq_size = lax.axis_size("seq")
     fsdp_size = lax.axis_size("fsdp")
     seq_index = lax.axis_index("seq")
@@ -183,7 +215,7 @@
     ).reshape(fsdp_size * panel_padded, pixel_width + 6)
     piece = lax.psum_scatter(stacked, ("fsdp", "seq"), scatter_dimension=0, tiled=True)
     grad_scale = 1.0 / math.sqrt(tokens * seq_size * fsdp_size)
-    summed = lax.all_gather(piece * grad_scale, "seq", axis=0, tiled=True)[:panel]
+    summed = convert_ways(piece * grad_scale, "seq", 0)[:panel]
     grad_weight = summed[:, :pixel_width].astype(jnp.bfloat16)
     grad_channels = summed[:, pixel_width:].T
     return (features[None], grad_rows[None], grad_weight, grad_channels)

time: 1610 us -> 1630 us (1.012)
  the two profiles are of different devices: /device:TPU:1 before, /device:TPU:30 now
where the time goes in v1:
time: 1630 us
  waiting for transfers between devices  1330 us (82%)
  starting transfers between devices  105 us (6%)
  other arithmetic  79.6 us (5%)
  local copies, waits for them, and re-layouts  70.4 us (4%)
  matrix products  29.6 us (2%)
    reduce_scatter x1, waiting for transfers between devices, shards(): lax.psum_scatter(stacked, ('fsdp', 'seq'), scatter_dimension=0, tiled=True)  1280 us
    ppermute x8, starting transfers between devices, convert_ways(): jax.lax.ppermute(everything[-1] if everything else local_x, chip_axis, pi...  77.7 us
  transfers between devices with their start and end apart: 23, of which 14 were waited for; matrix products, arithmetic and copies ran while one was open for 4% of the time, Pallas kernels for 0%

profile of v1, /device:TPU:30, one launch (start us, length us, event | category | flops | bytes accessed | tf_op | source)
XLA Modules:
  0.0 1627.9 jit_solution(6168049221587742807)
XLA Ops:
  7.2 0.7 broadcast_in_dim.26
  8.0 0.8 copy.24
  8.8 1.9 concatenate.24
  12.1 0.9 convert_reduce_fusion.1
  15.0 7.1 all-to-all-start
  22.3 1.8 broadcast_in_dim.21
  24.1 6.9 scatter_fusion
  31.0 7.2 all-to-all-start.1
  39.0 0.7 gather_fusion.5
  39.7 0.7 gather_fusion.1
  40.5 0.7 gather_fusion.2
  41.2 0.7 gather_fusion.3
  41.9 0.7 gather_fusion.4
  44.0 0.7 gather_fusion.8
  45.9 23.6 %all-to-all-done.1 = bf16[32,32,1176]{2,1,0:T(8,128)(2,1)} async-done(((bf16[32,32,1176]{2,1,0:T(8,128)(2,1)}), bf16[32,32,1176]{2,1,0:T(8,128)(2,1)}, u32[]{:S(2)}, u32[]{:S(2)}) %all-to-all-start.1) | async-done | bytes 2408480 | tf_op jit(solution)/shard_map/all_to_all | solution.py:148
  69.7 4.7 scatter_fusion.1
  74.5 1.6 slice_bitcast_fusion
  76.8 4.3 slice_reduce_fusion.4
  81.2 5.5 multiply_reduce_fusion.2
  86.7 1.3 multiply_convert_fusion
  88.1 1.6 collective-permute-start
  89.6 4.7 collective-permute-start.1
  94.5 0.8 broadcast_multiply_fusion
  95.3 0.9 broadcast_multiply_fusion.1
  96.2 0.9 broadcast_multiply_fusion.2
  97.1 0.9 broadcast_multiply_fusion.3
  97.9 3.7 collective-permute-done
  101.6 1.2 collective-permute-done.1
  102.8 10.2 convert_multiply_fusion
  113.1 4.3 reduce_sum.141
  117.6 2.0 fusion.56
  119.5 5.2 collective-permute-start.2
  124.7 1.3 collective-permute-start.3
  126.0 15.1 convert_multiply_fusion.1
  141.1 4.3 reduce_sum.139
  145.6 4.4 reduce_sum.137
  150.1 4.4 reduce_sum.133
  154.6 4.4 reduce_sum.135
  159.2 10.2 fusion.13
  169.5 2.1 multiply_reduce_fusion
  171.6 9.6 fusion.10
  181.3 13.7 pad_add_fusion
  195.1 18.8 %copy.25 = f32[3584,1182]{1,0:T(8,128)} copy(f32[3584,1182]{0,1:T(8,128)} %pad_add_fusion) | data formatting | bytes 33890304 | tf_op jit(solution)/shard_map/add | solution.py:209
  213.9 15.3 pad.14
  229.1 1277.6 %reduce-scatter.2.cloned.1.call-done = f32[16,1182]{1,0:T(8,128)} async-done(((f32[4096,1182]{1,0:T(8,128)}), f32[16,1182]{1,0:T(8,128)}) %reduce-scatter.2.cloned.1.call-update) | async-done | bytes 75664 | tf_op jit(solution)/shard_map/reduce_scatter | solution.py:216
  1506.7 0.9 broadcast_multiply_fusion.10
  1507.6 37.4 %collective-permute-start.4 = (f32[16,1182]{1,0:T(8,128)S(1)}, f32[16,1182]{1,0:T(8,128)S(1)}, u32[]{:S(2)}, u32[]{:S(2)}) collective-permute-start(f32[16,1182]{1,0:T(8,128)S(1)} %broadcast_multiply_fusion.10), channel_id=1, source_target_pairs={{0,16},{16,32},{32,48},{48,64},{64,80},{80,96},{96,112},{112,128},... | collective-permute-start | bytes 226952 | tf_op jit(solution)/shard_map/ppermute | solution.py:109
  1545.0 2.1 collective-permute-done.4
  1547.1 5.7 collective-permute-start.5
  1552.8 2.3 collective-permute-done.5
  1555.1 5.8 collective-permute-start.6
  1561.1 2.0 collective-permute-done.6
  1563.1 5.8 collective-permute-start.7
  1568.9 2.1 collective-permute-done.7
  1571.0 5.7 collective-permute-start.8
  1576.7 2.1 collective-permute-done.8
  1578.7 5.9 collective-permute-start.9
  1584.8 1.9 collective-permute-done.9
  1586.7 5.7 collective-permute-start.10
  1592.5 2.0 collective-permute-done.10
  1594.5 5.7 collective-permute-start.11
  1600.2 10.4 fusion.23
  1610.9 7.5 collective-permute-done.18
  1619.2 0.9 slice.300
  (124 shorter events, 10.9 us)
Async XLA Ops:
  7.2 31.1 %copy-start = (s32[1,272]{1,0:T(1,128)S(1)}, s32[1,272]{1,0:T(1,128)}, u32[]{:S(2)}) copy-start(s32[1,272]{1,0:T(1,128)} %param.9) | copy-start | bytes 3268
  7.2 67.3 %all-gather.2.cloned.1.call-start = ((), (), s32[]{:S(2)}) async-start(), calls=%async_computation.3 | async-start | bytes 9748480 | tf_op jit(solution)/shard_map/all_gather | solution.py:161
  15.0 16.0 all-to-all-start
  31.0 38.5 %all-to-all-start.1 = ((bf16[32,32,1176]{2,1,0:T(8,128)(2,1)}), bf16[32,32,1176]{2,1,0:T(8,128)(2,1)}, u32[]{:S(2)}, u32[]{:S(2)}) async-start(bf16[32,32,1176]{2,1,0:T(8,128)(2,1)} %scatter_fusion), calls=%async_computation.1 | async-start | bytes 5242880 | tf_op jit(solution)/shard_map/all_to_all | solution.py:148
  38.2 1468.5 %reduce-scatter.2.cloned.1.call-start = ((), (), s32[]{:S(2)}) async-start(), calls=%async_computation.4 | async-start | bytes 21053440 | tf_op jit(solution)/shard_map/reduce_scatter | solution.py:216
  74.5 6.7 copy-start.6
  86.6 9.5 copy-start.2
  86.7 16.2 copy-start.4
  88.0 25.1 %copy-start.3 = (bf16[544,3584]{1,0:T(8,128)(2,1)}, bf16[544,3584]{1,0:T(8,128)(2,1)S(1)}, u32[]{:S(2)}) copy-start(bf16[544,3584]{1,0:T(8,128)(2,1)S(1)} %multiply_convert_fusion) | copy-start | bytes 11698180
  88.1 13.6 collective-permute-start
  89.6 13.2 collective-permute-start.1
  119.5 39.6 %collective-permute-start.2 = (bf16[64,3584]{1,0:T(8,128)(2,1)}, bf16[64,3584]{1,0:T(8,128)(2,1)}, u32[]{:S(2)}, u32[]{:S(2)}) collective-permute-start(bf16[64,3584]{1,0:T(8,128)(2,1)} %get-tuple-element.40), channel_id=1, source_target_pairs={{16,0},{32,16},{48,32},{64,48},{80,64},{96,80},{112,96},{128,112},... | collective-permute-start | bytes 1376264 | tf_op jit(solution)/shard_map/ppermute | solution.py:34
  124.7 34.5 %collective-permute-start.3 = (bf16[64,3584]{1,0:T(8,128)(2,1)S(1)}, bf16[64,3584]{1,0:T(8,128)(2,1)}, u32[]{:S(2)}, u32[]{:S(2)}) collective-permute-start(bf16[64,3584]{1,0:T(8,128)(2,1)S(1)} %get-tuple-element.41), channel_id=1, source_target_pairs={{0,16},{16,32},{32,48},{48,64},{64,80},{80,96},{96,112},{112,128},... | collective-permute-start | bytes 1376264 | tf_op jit(solution)/shard_map/ppermute | solution.py:32
  159.0 10.4 slice-start
  159.2 10.3 slice-start.1
  1507.6 39.4 %collective-permute-start.4 = (f32[16,1182]{1,0:T(8,128)S(1)}, f32[16,1182]{1,0:T(8,128)S(1)}, u32[]{:S(2)}, u32[]{:S(2)}) collective-permute-start(f32[16,1182]{1,0:T(8,128)S(1)} %broadcast_multiply_fusion.10), channel_id=1, source_target_pairs={{0,16},{16,32},{32,48},{48,64},{64,80},{80,96},{96,112},{112,128},... | collective-permute-start | bytes 226952 | tf_op jit(solution)/shard_map/ppermute | solution.py:109
  1547.1 8.0 collective-permute-start.5
  1552.8 8.3 collective-permute-start.12
  1555.1 8.0 collective-permute-start.6
  1561.1 7.8 collective-permute-start.13
  1563.1 7.9 collective-permute-start.7
  1568.9 7.8 collective-permute-start.14
  1571.0 7.8 collective-permute-start.8
  1576.7 8.0 collective-permute-start.15
  1578.7 8.0 collective-permute-start.9
  1584.7 7.8 collective-permute-start.16
  1586.7 7.8 collective-permute-start.10
  1592.4 18.3 %copy-start.5 = (f32[16,1182]{1,0:T(8,128)S(1)}, f32[16,1182]{1,0:T(8,128)}, u32[]{:S(2)}) copy-start(f32[16,1182]{1,0:T(8,128)} %reduce-scatter.2.cloned.1.call-done) | copy-start | bytes 226948
  1592.5 18.1 %collective-permute-start.17 = (f32[16,1182]{1,0:T(8,128)S(1)}, f32[16,1182]{1,0:T(8,128)S(1)}, u32[]{:S(2)}, u32[]{:S(2)}) collective-permute-start(f32[16,1182]{1,0:T(8,128)S(1)} %collective-permute-done.16), channel_id=1, source_target_pairs={{16,0},{32,16},{48,32},{64,48},{80,64},{96,80},{112,96},{128,112},... | collective-permute-start | bytes 226952 | tf_op jit(solution)/shard_map/ppermute | solution.py:114
  1594.5 16.1 collective-permute-start.11
  1600.2 20.6 %copy-start.1 = (s32[1,272]{1,0:T(1,128)S(1)}, s32[1,272]{1,0:T(1,128)}, u32[]{:S(2)}) copy-start(s32[1,272]{1,0:T(1,128)} %param.9) | copy-start | bytes 3268
  1610.6 7.8 collective-permute-start.18
Sparse Core Ops, SparseCore 0:
  10.9 62.2 all-gather.1
  229.3 1277.4 reduce-scatter.1
